TPU v7x, 128 devices: a whole 4x4x4 slice. The times are simulated.
128 devices in a mesh: rows: 16 (over y, z), seq: 8 (over x, core).
Axes of the slice: x: 4, y: 4, z: 4, core: 2. Of those that a mesh axis runs over, the one named last changes fastest.
Arguments:
- residual_in: bfloat16 [16, 2048, 3200], P('rows', 'seq'), may hold values from -6 to 6
- norm_gain: float32 [3200], replicated, may hold values from 0.1 to 1.9
- qkv_weight: bfloat16 [3200, 6144], P(None, 'seq')
- qk_gain: float32 [2, 2048], P(None, 'seq')
- out_weight: bfloat16 [2048, 3200], P('seq'), may hold values from -0.125 to 0.125
- layer_scale: float32 [3200], replicated, may hold values from 1 to 6
- segment_ids: int32 [16, 2048], P('rows', 'seq'), may hold values from 0 to 2, as said below
- pad_mask: int32 [16, 2048], P('rows', 'seq'), may hold values from 0 to 1, as said below
- ln_weight: float32 [12800], replicated, may hold values from 0.1 to 1.9
- ln_bias: float32 [12800], replicated, may hold values from -3 to 3
- fc_weight: bfloat16 [12800, 6144], P('rows'), may hold values from -0.0546875 to 0.0546875
- fc_bias: float32 [6144], replicated, may hold values from -3 to 3
- owner: int32 [16], replicated, may hold values from 0 to 15, each once
Outputs:
- features: bfloat16 [16, 512, 6144], P('rows', 'seq')
Inputs may be any that keep to these rules, and one draw needn't show every extreme that they name: `segment_ids`: within a row, segment ids never fall and change only at multiples of 1024 tokens; picture tokens carry ids below 2, padding tokens carry 2 and stand at the end of the row; the first tile is never padding. pad_mask is 0 exactly where segment_ids equals 2. `owner`: each index of rows owns exactly one row.
All inputs are finite; a program needn't handle non-finite values.
Results may differ from a plain program's by a relative error of at most 0.025.
Values may be sent and summed in bfloat16 or wider, within the bound.
A program may use at most 128 MiB of HBM per device.

v0:
```python
import jax
import jax.numpy as jnp
from jax import lax
from jax.sharding import PartitionSpec as P

D = 3200
HEAD_DIM = 128
HEADS = 16
GRID = 32
MASK_SHIFT = 1000000.0


def attend_dense(query_norm, key_norm, value_half, row_segments, block_len, scale):
    length, heads_here = (query_norm.shape[0], query_norm.shape[1])
    block_count = length // block_len

    def one_block(packed):
        query_block, query_seg = packed
        scores = (
            jnp.einsum("qhd,khd->hqk", query_block, key_norm, preferred_element_type=jnp.float32)
            * scale
        )
        same_seg = (query_seg[:, None] == row_segments[None, :])[None]
        scores = jnp.where(same_seg, scores, -1e30)
        peak_val = jnp.max(scores, axis=-1, keepdims=True)
        exp_terms = jnp.exp(scores - peak_val)
        probs = (exp_terms / jnp.sum(exp_terms, axis=-1, keepdims=True)).astype(jnp.bfloat16)
        return jnp.einsum(
            "hqk,khd->qhd", probs, value_half, preferred_element_type=jnp.float32
        ).astype(jnp.bfloat16)

    blocks_out = lax.map(
        one_block,
        (
            query_norm.reshape(block_count, block_len, heads_here, HEAD_DIM),
            row_segments.reshape(block_count, block_len),
        ),
    )
    return blocks_out.reshape(length, heads_here * HEAD_DIM)


def per_device(
    residual_in,
    norm_gain,
    qkv_weight,
    qk_gain,
    out_weight,
    layer_scale,
    segment_ids,
    pad_mask,
    ln_weight,
    ln_bias,
    fc_weight,
    fc_bias,
    owner,
):
    seq_count = lax.axis_size("seq")
    seq_me = lax.axis_index("seq")
    tokens = residual_in[0].astype(jnp.float32)
    shard_rows = tokens.shape[0]
    normed = (
        tokens * lax.rsqrt(jnp.mean(tokens * tokens, axis=-1, keepdims=True) + 1e-06) * norm_gain
    ).astype(jnp.bfloat16)
    row_tokens = lax.all_gather(normed, "seq", axis=0, tiled=True)
    length = row_tokens.shape[0]
    heads_here = qkv_weight.shape[1] // (3 * HEAD_DIM)
    projected = jnp.dot(row_tokens, qkv_weight, preferred_element_type=jnp.float32).reshape(
        length, heads_here, 3, HEAD_DIM
    )
    query_raw = projected[:, :, 0]
    key_raw = projected[:, :, 1]
    value_half = projected[:, :, 2].astype(jnp.bfloat16)
    seg_spread = lax.dynamic_update_slice_in_dim(
        jnp.zeros((length,), jnp.float32),
        segment_ids[0].astype(jnp.float32),
        seq_me * shard_rows,
        0,
    )
    stats = lax.psum(
        jnp.stack(
            [
                jnp.sum(query_raw * query_raw, axis=(1, 2)),
                jnp.sum(key_raw * key_raw, axis=(1, 2)),
                seg_spread,
            ]
        ),
        "seq",
    )
    query_sq, key_sq, row_segments = (stats[0], stats[1], stats[2])
    norm_width = HEADS * HEAD_DIM
    gain_pair = qk_gain.reshape(2, heads_here, HEAD_DIM)
    query_norm = (
        query_raw * lax.rsqrt(query_sq / norm_width + 1e-06)[:, None, None] * gain_pair[0]
    ).astype(jnp.bfloat16)
    key_norm = (
        key_raw * lax.rsqrt(key_sq / norm_width + 1e-06)[:, None, None] * gain_pair[1]
    ).astype(jnp.bfloat16)
    block_len = min(512, length)
    scale = HEAD_DIM ** (-0.5)
    attended = attend_dense(query_norm, key_norm, value_half, row_segments, block_len, scale)
    group_width = attended.shape[1]
    own_heads = lax.all_to_all(attended.reshape(seq_count, shard_rows, group_width), "seq", 0, 0)
    full_out_weight = lax.all_gather(out_weight, "seq", axis=0, tiled=False)
    group_terms = jnp.einsum(
        "gtc,gcd->gtd", own_heads, full_out_weight, preferred_element_type=jnp.float32
    ).astype(jnp.bfloat16)
    attn = jnp.sum(group_terms.astype(jnp.float32), axis=0)
    hidden = tokens + layer_scale * attn
    half_grid = GRID // 2
    lines = shard_rows // (2 * GRID)
    merged_count = shard_rows // 4
    merged = jnp.transpose(hidden.reshape(lines, 2, half_grid, 2, D), (0, 2, 1, 3, 4)).reshape(
        merged_count, 4 * D
    )
    centre = merged - jnp.mean(merged, axis=-1, keepdims=True)
    spread = jnp.mean(centre * centre, axis=-1, keepdims=True)
    merged_norm = (centre * lax.rsqrt(spread + 1e-05) * ln_weight + ln_bias).astype(jnp.bfloat16)
    merged_mask = (
        pad_mask[0]
        .reshape(lines, 2, half_grid, 2)[:, 0, :, 0]
        .reshape(merged_count)
        .astype(jnp.float32)
    )
    row_count = lax.axis_size("rows")
    row_me = lax.axis_index("rows")
    slabs = lax.all_to_all(merged_norm, "rows", split_axis=1, concat_axis=0, tiled=True)
    owner_hot = (owner[None, :] == jnp.arange(row_count, dtype=jnp.int32)[:, None]).astype(
        jnp.bfloat16
    )
    ordered = jnp.einsum(
        "jp,pms->jms",
        owner_hot,
        slabs.reshape(row_count, merged_count, -1),
        preferred_element_type=jnp.float32,
    ).astype(jnp.bfloat16)
    ordered = ordered.reshape(row_count * merged_count, -1)
    partial = jnp.dot(ordered, fc_weight, preferred_element_type=jnp.float32).reshape(
        row_count, merged_count, -1
    )
    own_slot = (jnp.arange(row_count, dtype=jnp.int32) == owner[row_me]).astype(jnp.float32)
    shift = own_slot[:, None] * ((merged_mask - 1.0) * MASK_SHIFT)[None, :]
    partial = (partial + shift[:, :, None]).astype(jnp.bfloat16)
    summed = lax.psum_scatter(
        partial.reshape(row_count * merged_count, -1), "rows", scatter_dimension=0, tiled=True
    ).astype(jnp.float32)
    result = jax.nn.gelu(summed + fc_bias, approximate=False)
    return result.astype(jnp.bfloat16)[None]


def solution(mesh):
    return jax.shard_map(
        per_device,
        mesh=mesh,
        in_specs=(
            P("rows", "seq", None),
            P(),
            P(None, "seq"),
            P(None, "seq"),
            P("seq", None),
            P(),
            P("rows", "seq"),
            P("rows", "seq"),
            P(),
            P(),
            P("rows", None),
            P(),
            P(),
        ),
        out_specs=P("rows", "seq", None),
        check_vma=False,
    )
```

profile of v0, /device:TPU:1, one launch (start us, length us, event | category | flops | bytes accessed | tf_op | source)
XLA Modules:
  0.0 404.6 jit_solution(10836090393352335551)
XLA Ops:
  11.7 72.5 %all-gather.4.cloned.1.call-done = bf16[2048,3200]{1,0:T(8,128)(2,1)} async-done(((bf16[256,3200]{1,0:T(8,128)(2,1)}), bf16[2048,3200]{1,0:T(8,128)(2,1)}) %all-gather.4.cloned.1.call-update) | async-done | bytes 13107216 | tf_op jit(solution)/shard_map/all_gather | solution.py:64
  84.2 15.7 %fusion.74 = f32[2048,768]{0,1:T(8,128)S(1)} fusion(bf16[2048,3200]{1,0:T(8,128)(2,1)} %all-gather.4.cloned.1.call-done, bf16[3200,768]{1,0:T(8,128)(2,1)} %param.17), kind=kOutput, calls=%fused_computation.97 | convolution fusion | flops 10066329600 | bytes 24313856 | tf_op jit(solution)/shard_map/dot_general | solution.py:67
  109.3 22.6 %psum.7 = f32[3,2048]{1,0:T(4,128)S(1)} all-reduce(f32[3,2048]{1,0:T(4,128)S(1)} %pad_maximum_fusion), channel_id=1, replica_groups=mesh['rows'=16,'seq'=8] {'seq'}, use_global_device_ids=true, to_apply=%region_3.0 | all-reduce | flops 6144 | bytes 49152 | tf_op jit(solution)/shard_map/psum | solution.py:79
  133.3 3.0 multiply_convert_fusion
  137.6 53.7 %while.10 = (s32[]{:T(128)}, bf16[4,512,2,128]{3,2,1,0:T(2,128)(2,1)S(1)}, f32[4,512]{1,0:T(4,128)S(1)}, f32[1,2048]{1,0:T(1,128)S(1)}, bf16[4,512,2,128]{3,1,0,...) while((s32[]{:T(128)}, ...), condition=%wide.region_7.8_spmd, body=%wide.region_4.7_spmd.sunk | while | flops 1087506432 | bytes 26237560 | solution.py:32
  138.3 7.8 %fusion.90 = (f32[2,512]{1,0:T(2,128)S(1)}, f32[2,512,2048]{2,1,0:T(8,128)}) fusion(pred[512,2048]{1,0:T(8,128)(4,1)S(1)} %broadcast_compare_fusion.2, bf16[2048,2,128]{2,0,1:T(8,128)(2,1)} %get-tuple-element.158, bf16[4,512,2,128]{3,1,0,2:T(8,128)(2,1)} %get-tuple-element.157, s32[]{:T(128)} %get-tuple-element.145), kind=kOutput, calls=%fused_computation.94.clone.1 | convolution fusion | flops 545261568 | bytes 10752512 | tf_op jit(solution)/shard_map/while/body/eval_jaxpr/sub | solution.py:26
  146.1 4.7 %fusion.91 = bf16[1,512,2,128]{3,1,2,0:T(8,128)(2,1)S(1)} fusion(bf16[2048,2,128]{2,0,1:T(8,128)(2,1)S(1)} %copy-done.5, f32[2,512,2048]{2,1,0:T(8,128)} %get-tuple-element.135, f32[2,512]{1,0:T(2,128)S(1)} %get-tuple-element.136), kind=kOutput, calls=%fused_computation.11.clone.1 | convolution fusion | flops 541196288 | bytes 9703424 | tf_op jit(solution)/shard_map/while/body/eval_jaxpr/hqk,khd->qhd/dot_general | solution.py:28
  151.8 7.7 %fusion.90 = (f32[2,512]{1,0:T(2,128)S(1)}, f32[2,512,2048]{2,1,0:T(8,128)}) fusion(pred[512,2048]{1,0:T(8,128)(4,1)S(1)} %broadcast_compare_fusion.2, bf16[2048,2,128]{2,0,1:T(8,128)(2,1)} %get-tuple-element.158, bf16[4,512,2,128]{3,1,0,2:T(8,128)(2,1)} %get-tuple-element.157, s32[]{:T(128)} %get-tuple-element.145), kind=kOutput, calls=%fused_computation.94.clone.1 | convolution fusion | flops 545261568 | bytes 10752512 | tf_op jit(solution)/shard_map/while/body/eval_jaxpr/sub | solution.py:26
  159.5 4.7 %fusion.91 = bf16[1,512,2,128]{3,1,2,0:T(8,128)(2,1)S(1)} fusion(bf16[2048,2,128]{2,0,1:T(8,128)(2,1)S(1)} %copy-done.5, f32[2,512,2048]{2,1,0:T(8,128)} %get-tuple-element.135, f32[2,512]{1,0:T(2,128)S(1)} %get-tuple-element.136), kind=kOutput, calls=%fused_computation.11.clone.1 | convolution fusion | flops 541196288 | bytes 9703424 | tf_op jit(solution)/shard_map/while/body/eval_jaxpr/hqk,khd->qhd/dot_general | solution.py:28
  165.2 7.7 %fusion.90 = (f32[2,512]{1,0:T(2,128)S(1)}, f32[2,512,2048]{2,1,0:T(8,128)}) fusion(pred[512,2048]{1,0:T(8,128)(4,1)S(1)} %broadcast_compare_fusion.2, bf16[2048,2,128]{2,0,1:T(8,128)(2,1)} %get-tuple-element.158, bf16[4,512,2,128]{3,1,0,2:T(8,128)(2,1)} %get-tuple-element.157, s32[]{:T(128)} %get-tuple-element.145), kind=kOutput, calls=%fused_computation.94.clone.1 | convolution fusion | flops 545261568 | bytes 10752512 | tf_op jit(solution)/shard_map/while/body/eval_jaxpr/sub | solution.py:26
  172.9 4.7 %fusion.91 = bf16[1,512,2,128]{3,1,2,0:T(8,128)(2,1)S(1)} fusion(bf16[2048,2,128]{2,0,1:T(8,128)(2,1)S(1)} %copy-done.5, f32[2,512,2048]{2,1,0:T(8,128)} %get-tuple-element.135, f32[2,512]{1,0:T(2,128)S(1)} %get-tuple-element.136), kind=kOutput, calls=%fused_computation.11.clone.1 | convolution fusion | flops 541196288 | bytes 9703424 | tf_op jit(solution)/shard_map/while/body/eval_jaxpr/hqk,khd->qhd/dot_general | solution.py:28
  178.6 7.7 %fusion.90 = (f32[2,512]{1,0:T(2,128)S(1)}, f32[2,512,2048]{2,1,0:T(8,128)}) fusion(pred[512,2048]{1,0:T(8,128)(4,1)S(1)} %broadcast_compare_fusion.2, bf16[2048,2,128]{2,0,1:T(8,128)(2,1)} %get-tuple-element.158, bf16[4,512,2,128]{3,1,0,2:T(8,128)(2,1)} %get-tuple-element.157, s32[]{:T(128)} %get-tuple-element.145), kind=kOutput, calls=%fused_computation.94.clone.1 | convolution fusion | flops 545261568 | bytes 10752512 | tf_op jit(solution)/shard_map/while/body/eval_jaxpr/sub | solution.py:26
  186.3 4.7 %fusion.91 = bf16[1,512,2,128]{3,1,2,0:T(8,128)(2,1)S(1)} fusion(bf16[2048,2,128]{2,0,1:T(8,128)(2,1)S(1)} %copy-done.5, f32[2,512,2048]{2,1,0:T(8,128)} %get-tuple-element.135, f32[2,512]{1,0:T(2,128)S(1)} %get-tuple-element.136), kind=kOutput, calls=%fused_computation.11.clone.1 | convolution fusion | flops 541196288 | bytes 9703424 | tf_op jit(solution)/shard_map/while/body/eval_jaxpr/hqk,khd->qhd/dot_general | solution.py:28
  192.8 7.8 %all-to-all-start = ((bf16[8,256,256]{2,1,0:T(8,128)(2,1)}), bf16[8,256,256]{2,1,0:T(8,128)(2,1)S(1)}, u32[]{:S(2)}, u32[]{:S(2)}) async-start(bf16[8,256,256]{2,1,0:T(8,128)(2,1)} %reshape_reshape.3), calls=%async_computation | async-start | bytes 2097152 | tf_op jit(solution)/shard_map/all_to_all | solution.py:102
  203.7 12.1 %all-to-all-done = bf16[8,256,256]{2,1,0:T(8,128)(2,1)S(1)} async-done(((bf16[8,256,256]{2,1,0:T(8,128)(2,1)}), bf16[8,256,256]{2,1,0:T(8,128)(2,1)S(1)}, u32[]{:S(2)}, u32[]{:S(2)}) %all-to-all-start) | async-done | bytes 1048608 | tf_op jit(solution)/shard_map/all_to_all | solution.py:102
  215.7 10.6 %convert_reduce_fusion = f32[256,3200]{1,0:T(8,128)} fusion(bf16[8,256,256]{2,1,0:T(8,128)(2,1)S(1)} %all-to-all-done, bf16[8,256,3200]{2,1,0:T(8,128)(2,1)} %bitcast.99), kind=kOutput, calls=%fused_computation.24 | convolution fusion | flops 3374284800 | bytes 17432576 | tf_op jit(solution)/shard_map/gtc,gcd->gtd/dot_general | solution.py:104
  226.3 5.3 %reduce_sum.69 = f32[4,2,16,2,3200]{4,3,2,1,0:T(2,128)} reshape(f32[256,3200]{1,0:T(8,128)} %convert_reduce_fusion) | data formatting | bytes 6553600 | tf_op jit(solution)/shard_map/reduce_sum | solution.py:107
  231.7 4.2 %fusion.66 = (f32[4,16]{1,0:T(4,128)S(1)}, f32[4,16,2,2,3200]{4,3,1,2,0:T(2,128)S(1)}) fusion(f32[4,2,16,2,3200]{4,3,2,1,0:T(2,128)S(1)} %copy-done.3, f32[4,2,16,2,3200]{4,3,2,1,0:T(2,128)} %reduce_sum.69, f32[3200]{0:T(1024)S(1)} %copy-done.9), kind=kLoop, calls=%fused_computation.93 | loop fusion | flops 2457536 | bytes 9843456 | tf_op jit(solution)/shard_map/reduce_sum | solution.py:115
  238.3 4.5 %reshape.212 = f32[64,16,800]{2,1,0:T(8,128)} reshape(f32[4,16,2,2,3200]{4,3,2,1,0:T(2,128)S(1)} %copy.36) | data formatting | bytes 6553600 | tf_op jit(solution)/shard_map/reshape | solution.py:112
  247.1 7.0 %all-to-all-start.1 = ((bf16[64,16,800]{2,0,1:T(8,128)(2,1)}), bf16[64,16,800]{2,0,1:T(8,128)(2,1)S(1)}, u32[]{:S(2)}, u32[]{:S(2)}) async-start(bf16[64,16,800]{2,0,1:T(8,128)(2,1)} %copy.37), calls=%async_computation.1 | async-start | bytes 3670016 | tf_op jit(solution)/shard_map/all_to_all | solution.py:126
  257.0 20.2 %all-to-all-done.1 = bf16[64,16,800]{2,0,1:T(8,128)(2,1)S(1)} async-done(((bf16[64,16,800]{2,0,1:T(8,128)(2,1)}), bf16[64,16,800]{2,0,1:T(8,128)(2,1)S(1)}, u32[]{:S(2)}, u32[]{:S(2)}) %all-to-all-start.1) | async-done | bytes 1638432 | tf_op jit(solution)/shard_map/all_to_all | solution.py:126
  278.5 19.2 %add_convert_fusion = bf16[16,64,6144]{2,1,0:T(8,128)(2,1)} fusion(f32[16,64]{1,0:T(8,128)S(1)} %broadcast_multiply_fusion, bf16[800,6144]{1,0:T(8,128)(2,1)} %param.25, bf16[16,64,800]{2,0,1:T(8,128)(2,1)S(1)} %fusion.38), kind=kOutput, calls=%fused_computation.25 | convolution fusion | flops 10078912512 | bytes 24055808 | tf_op jit(solution)/shard_map/dot_general | solution.py:137
  297.8 95.1 %reduce-scatter.2.cloned.1.call-done = bf16[64,6144]{1,0:T(8,128)(2,1)} async-done(((bf16[1024,6144]{1,0:T(8,128)(2,1)}), bf16[64,6144]{1,0:T(8,128)(2,1)}) %reduce-scatter.2.cloned.1.call-update) | async-done | bytes 786448 | tf_op jit(solution)/shard_map/reduce_scatter | solution.py:143
  392.9 5.2 %fusion.54 = bf16[1,64,6144]{2,1,0:T(8,128)(2,1)} fusion(bf16[64,6144]{1,0:T(8,128)(2,1)} %reduce-scatter.2.cloned.1.call-done, f32[6144]{0:T(1024)S(1)} %copy-done.8), kind=kLoop, calls=%fused_computation.70 | loop fusion | flops 26345472 | bytes 1597440 | tf_op jit(solution)/shard_map/broadcast_in_dim | solution.py:147
  (93 shorter events, 36.5 us)
Async XLA Ops:
  6.5 2.0 copy-start.1
  6.5 77.7 %all-gather.4.cloned.1.call-start = ((), (), s32[]{:S(2)}) async-start(), calls=%async_computation.3 | async-start | bytes 14745600 | tf_op jit(solution)/shard_map/all_gather | solution.py:64
  10.9 0.8 copy-start.11
  10.9 0.8 copy-start.10
  10.9 192.8 %all-gather.6.cloned.1.call-start = ((), (), s32[]{:S(2)}) async-start(), calls=%async_computation.5 | async-start | bytes 14745600 | tf_op jit(solution)/shard_map/all_gather | solution.py:103
  107.3 1.6 copy-start
  136.3 1.3 copy-start.4
  138.3 7.8 %copy-start.5 = (bf16[2048,2,128]{2,0,1:T(8,128)(2,1)S(1)}, bf16[2048,2,128]{2,0,1:T(8,128)(2,1)}, u32[]{:S(2)}) copy-start(bf16[2048,2,128]{2,0,1:T(8,128)(2,1)} %get-tuple-element.159) | copy-start | bytes 3145732 | tf_op jit(solution)/shard_map/while
  151.7 7.8 %copy-start.5 = (bf16[2048,2,128]{2,0,1:T(8,128)(2,1)S(1)}, bf16[2048,2,128]{2,0,1:T(8,128)(2,1)}, u32[]{:S(2)}) copy-start(bf16[2048,2,128]{2,0,1:T(8,128)(2,1)} %get-tuple-element.159) | copy-start | bytes 3145732 | tf_op jit(solution)/shard_map/while
  165.2 7.8 %copy-start.5 = (bf16[2048,2,128]{2,0,1:T(8,128)(2,1)S(1)}, bf16[2048,2,128]{2,0,1:T(8,128)(2,1)}, u32[]{:S(2)}) copy-start(bf16[2048,2,128]{2,0,1:T(8,128)(2,1)} %get-tuple-element.159) | copy-start | bytes 3145732 | tf_op jit(solution)/shard_map/while
  178.6 7.8 %copy-start.5 = (bf16[2048,2,128]{2,0,1:T(8,128)(2,1)S(1)}, bf16[2048,2,128]{2,0,1:T(8,128)(2,1)}, u32[]{:S(2)}) copy-start(bf16[2048,2,128]{2,0,1:T(8,128)(2,1)} %get-tuple-element.159) | copy-start | bytes 3145732 | tf_op jit(solution)/shard_map/while
  191.3 9.3 %copy-start.2 = (bf16[1,256,3200]{2,1,0:T(8,128)(2,1)S(1)}, bf16[1,256,3200]{2,1,0:T(8,128)(2,1)}, u32[]{:S(2)}) copy-start(bf16[1,256,3200]{2,1,0:T(8,128)(2,1)} %param.15) | copy-start | bytes 4915204
  192.8 22.9 %all-to-all-start = ((bf16[8,256,256]{2,1,0:T(8,128)(2,1)}), bf16[8,256,256]{2,1,0:T(8,128)(2,1)S(1)}, u32[]{:S(2)}, u32[]{:S(2)}) async-start(bf16[8,256,256]{2,1,0:T(8,128)(2,1)} %reshape_reshape.3), calls=%async_computation | async-start | bytes 2097152 | tf_op jit(solution)/shard_map/all_to_all | solution.py:102
  200.6 2.8 copy-start.6
  200.6 2.9 copy-start.7
  226.3 5.3 %copy-start.3 = (f32[4,2,16,2,3200]{4,3,2,1,0:T(2,128)S(1)}, f32[4,2,16,2,3200]{4,3,2,1,0:T(2,128)}, u32[]{:S(2)}) copy-start(f32[4,2,16,2,3200]{4,3,2,1,0:T(2,128)} %reshape.214) | copy-start | bytes 9830404
  226.3 5.3 %copy-start.9 = (f32[3200]{0:T(1024)S(1)}, f32[3200]{0:T(1024)}, u32[]{:S(2)}) copy-start(f32[3200]{0:T(1024)} %param.20) | copy-start | bytes 38404
  247.1 7.6 %copy-start.12 = (s32[1,256]{1,0:T(1,128)S(1)}, s32[1,256]{1,0:T(1,128)}, u32[]{:S(2)}) copy-start(s32[1,256]{1,0:T(1,128)} %param.22) | copy-start | bytes 3076
  247.1 8.6 %copy-start.13 = (s32[16]{0:T(128)S(1)}, s32[16]{0:T(128)}, u32[]{:S(2)}) copy-start(s32[16]{0:T(128)} %param.27) | copy-start | bytes 196
  247.1 30.1 %all-to-all-start.1 = ((bf16[64,16,800]{2,0,1:T(8,128)(2,1)}), bf16[64,16,800]{2,0,1:T(8,128)(2,1)S(1)}, u32[]{:S(2)}, u32[]{:S(2)}) async-start(bf16[64,16,800]{2,0,1:T(8,128)(2,1)} %copy.37), calls=%async_computation.1 | async-start | bytes 3670016 | tf_op jit(solution)/shard_map/all_to_all | solution.py:126
  254.2 138.7 %reduce-scatter.2.cloned.1.call-start = ((), (), s32[]{:S(2)}) async-start(), calls=%async_computation.4 | async-start | bytes 13369344 | tf_op jit(solution)/shard_map/reduce_scatter | solution.py:143
  297.7 95.1 %copy-start.8 = (f32[6144]{0:T(1024)S(1)}, f32[6144]{0:T(1024)}, u32[]{:S(2)}) copy-start(f32[6144]{0:T(1024)} %param.26) | copy-start | bytes 73732
Sparse Core Ops, SparseCore 0:
  11.0 73.1 all-gather.3
  85.9 70.2 all-gather.5
  297.9 94.9 reduce-scatter.1
where the time goes:
time: 405 us
  waiting for transfers between devices  201 us (50%)
  matrix products  96.5 us (24%)
  local copies, waits for them, and re-layouts  29 us (7%)
  other arithmetic  27.6 us (7%)
  blocking collectives  22.6 us (6%)
  starting transfers between devices  14.9 us (4%)
  between operations  13.3 us (3%)
    reduce_scatter x1, waiting for transfers between devices, per_device(): lax.psum_scatter(partial.reshape(row_count * merged_count, -1), 'rows', s...  95.1 us
    all_gather x1, waiting for transfers between devices, per_device(): row_tokens = lax.all_gather(normed, 'seq', axis=0, tiled=True)  72.5 us
    sub x4, matrix products, one_block(): exp_terms = jnp.exp(scores - peak_val)  31 us
    psum x1, blocking collectives, per_device(): lax.psum(jnp.stack([jnp.sum(query_raw * query_raw, axis=(1, 2)), jnp.sum(...  22.6 us
    all_to_all x1, waiting for transfers between devices, per_device(): lax.all_to_all(merged_norm, 'rows', split_axis=1, concat_axis=0, tiled=True)  20.2 us
    dot_general x1, matrix products, per_device(): jnp.dot(ordered, fc_weight, preferred_element_type=jnp.float32)  19.2 us
    dot_general x4, matrix products, one_block(): jnp.einsum('hqk,khd->qhd', probs, value_half, preferred_element_type=jnp....  18.7 us
    dot_general x1, matrix products, per_device(): jnp.dot(row_tokens, qkv_weight, preferred_element_type=jnp.float32)  15.7 us
  transfers between devices with their start and end apart: 5, of which 4 were waited for; matrix products, arithmetic and copies ran while one was open for 22% of the time, Pallas kernels for 0%

commit v1 on v0

--- a/solution.py
+++ b/solution.py
@@ -61,7 +61,9 @@
     normed = (
         tokens * lax.rsqrt(jnp.mean(tokens * tokens, axis=-1, keepdims=True) + 1e-06) * norm_gain
     ).astype(jnp.bfloat16)
-    row_tokens = lax.all_gather(normed, "seq", axis=0, tiled=True)
+    row_tokens = jnp.concatenate(
+        lax.all_to_all(jnp.stack([normed] * lax.axis_size("seq")), "seq", 0, 0), axis=0
+    )
     length = row_tokens.shape[0]
     heads_here = qkv_weight.shape[1] // (3 * HEAD_DIM)
     projected = jnp.dot(row_tokens, qkv_weight, preferred_element_type=jnp.float32).reshape(

time: 405 us -> 541 us (1.34)
  waiting for transfers between devices: 201 us -> 317 us
  local copies, waits for them, and re-layouts: 29 us -> 40.3 us
  starting transfers between devices: 14.9 us -> 21.7 us
    all_to_all x0 -> x1, waiting for transfers between devices: none -> 189 us  [per_device(): lax.all_to_all(jnp.stack([normed] * lax.axis_size('seq')), 'seq', 0, 0)]
    all_gather x1 -> x0, waiting for transfers between devices: 72.5 us -> none  [per_device(): row_tokens = lax.all_gather(normed, 'seq', axis=0, tiled=True)]
    all_to_all x0 -> x1, starting transfers between devices: none -> 6.68 us  [per_device(): lax.all_to_all(jnp.stack([normed] * lax.axis_size('seq')), 'seq', 0, 0)]
    another operation x0 -> x1, local copies, waits for them, and re-layouts: none -> 6.38 us  [per_device(): jnp.stack([normed] * lax.axis_size('seq'))]
  transfers between devices with their start and end apart: 5 -> 5, of which waited for: 4 -> 4; matrix products, arithmetic and copies ran while one was open for 22% -> 18% of each run, Pallas kernels for 0% -> 0%
where the time goes in v1:
time: 541 us; the launch traced here: 540 us
  waiting for transfers between devices  317 us (59%)
  matrix products  96.4 us (18%)
  local copies, waits for them, and re-layouts  40.3 us (7%)
  other arithmetic  29.6 us (5%)
  starting transfers between devices  21.7 us (4%)
  blocking collectives  21.2 us (4%)
  between operations  13.6 us (3%)
    all_to_all x1, waiting for transfers between devices, per_device(): lax.all_to_all(jnp.stack([normed] * lax.axis_size('seq')), 'seq', 0, 0)  189 us
    reduce_scatter x1, waiting for transfers between devices, per_device(): lax.psum_scatter(partial.reshape(row_count * merged_count, -1), 'rows', s...  95 us
    sub x4, matrix products, one_block(): exp_terms = jnp.exp(scores - peak_val)  30.6 us
    psum x1, blocking collectives, per_device(): lax.psum(jnp.stack([jnp.sum(query_raw * query_raw, axis=(1, 2)), jnp.sum(...  21.2 us
    all_to_all x1, waiting for transfers between devices, per_device(): lax.all_to_all(merged_norm, 'rows', split_axis=1, concat_axis=0, tiled=True)  20.2 us
    dot_general x4, matrix products, one_block(): jnp.einsum('hqk,khd->qhd', probs, value_half, preferred_element_type=jnp....  19.6 us
    dot_general x1, matrix products, per_device(): jnp.dot(ordered, fc_weight, preferred_element_type=jnp.float32)  19.2 us
    dot_general x1, matrix products, per_device(): jnp.dot(row_tokens, qkv_weight, preferred_element_type=jnp.float32)  15.1 us
  transfers between devices with their start and end apart: 5, of which 4 were waited for; matrix products, arithmetic and copies ran while one was open for 18% of the time, Pallas kernels for 0%

profile of v1, /device:TPU:1, one launch (start us, length us, event | category | flops | bytes accessed | tf_op | source)
XLA Modules:
  0.0 539.7 jit_solution(16324315204737987439)
XLA Ops:
  9.7 6.4 %stack.11 = bf16[8,256,3200]{2,1,0:T(8,128)(2,1)} broadcast(bf16[256,3200]{1,0:T(8,128)(2,1)S(1)} %fusion.37), dimensions={1,2} | broadcast | bytes 14745600 | tf_op jit(solution)/shard_map/stack | solution.py:65
  16.1 6.7 %all-to-all-start = ((bf16[8,256,3200]{2,1,0:T(8,128)(2,1)}), bf16[8,256,3200]{2,1,0:T(8,128)(2,1)}, u32[]{:S(2)}, u32[]{:S(2)}) async-start(bf16[8,256,3200]{2,1,0:T(8,128)(2,1)} %stack.11), calls=%async_computation | async-start | bytes 26214400 | tf_op jit(solution)/shard_map/all_to_all | solution.py:65
  23.5 7.5 %copy.27 = bf16[3200,768]{0,1:T(8,128)(2,1)} copy(bf16[3200,768]{1,0:T(8,128)(2,1)} %param.17) | data formatting | bytes 9830400 | tf_op args[2]
  31.1 188.8 %all-to-all-done = bf16[8,256,3200]{2,1,0:T(8,128)(2,1)} async-done(((bf16[8,256,3200]{2,1,0:T(8,128)(2,1)}), bf16[8,256,3200]{2,1,0:T(8,128)(2,1)}, u32[]{:S(2)}, u32[]{:S(2)}) %all-to-all-start) | async-done | bytes 13107232 | tf_op jit(solution)/shard_map/all_to_all | solution.py:65
  219.9 15.1 %fusion.72 = f32[2048,2,3,128]{3,0,2,1:T(8,128)S(1)} fusion(bf16[2048,3200,1,1]{1,0,3,2:T(8,128)(2,1)} %bitcast.9, bf16[2,3,128,3200]{3,2,1,0:T(8,128)(2,1)} %bitcast.83), kind=kOutput, calls=%fused_computation.96 | convolution fusion | flops 10066329600 | bytes 24313856 | tf_op jit(solution)/shard_map/dot_general | solution.py:69
  238.3 21.2 %psum.7 = f32[3,2048]{1,0:T(4,128)S(1)} all-reduce(f32[3,2048]{1,0:T(4,128)S(1)} %pad_maximum_fusion), channel_id=1, replica_groups=mesh['rows'=16,'seq'=8] {'seq'}, use_global_device_ids=true, to_apply=%region_3.0 | all-reduce | flops 6144 | bytes 49152 | tf_op jit(solution)/shard_map/psum | solution.py:81
  268.1 56.9 %while.10 = (s32[]{:T(128)}, bf16[4,512,2,128]{3,2,1,0:T(2,128)(2,1)}, f32[4,512]{1,0:T(4,128)S(1)}, f32[1,2048]{1,0:T(1,128)S(1)}, bf16[4,512,2,128]{3,1,2,0:T(...) while((s32[]{:T(128)}, bf16[4,512,2,128]{3,2,1,0:T(2,128)(2,1)}, ...), condition=%wide.region_7.8_spmd, body=%wide.region_4.7_spmd.sunk | while | flops 1087506432 | bytes 22043736 | solution.py:32
  268.8 7.7 %fusion.88 = (f32[2,512]{1,0:T(2,128)S(1)}, f32[2,512,2048]{2,1,0:T(8,128)}) fusion(pred[512,2048]{1,0:T(8,128)(4,1)S(1)} %broadcast_compare_fusion.2, bf16[2048,2,128]{2,0,1:T(8,128)(2,1)} %get-tuple-element.137, bf16[4,512,2,128]{3,1,2,0:T(8,128)(2,1)} %get-tuple-element.136, s32[]{:T(128)} %get-tuple-element.124), kind=kOutput, calls=%fused_computation.93.clone.1 | convolution fusion | flops 545261568 | bytes 10752512 | tf_op jit(solution)/shard_map/while/body/eval_jaxpr/sub | solution.py:26
  276.5 4.9 fusion.89
  283.0 7.7 %fusion.88 = (f32[2,512]{1,0:T(2,128)S(1)}, f32[2,512,2048]{2,1,0:T(8,128)}) fusion(pred[512,2048]{1,0:T(8,128)(4,1)S(1)} %broadcast_compare_fusion.2, bf16[2048,2,128]{2,0,1:T(8,128)(2,1)} %get-tuple-element.137, bf16[4,512,2,128]{3,1,2,0:T(8,128)(2,1)} %get-tuple-element.136, s32[]{:T(128)} %get-tuple-element.124), kind=kOutput, calls=%fused_computation.93.clone.1 | convolution fusion | flops 545261568 | bytes 10752512 | tf_op jit(solution)/shard_map/while/body/eval_jaxpr/sub | solution.py:26
  290.7 4.9 fusion.89
  297.3 7.7 %fusion.88 = (f32[2,512]{1,0:T(2,128)S(1)}, f32[2,512,2048]{2,1,0:T(8,128)}) fusion(pred[512,2048]{1,0:T(8,128)(4,1)S(1)} %broadcast_compare_fusion.2, bf16[2048,2,128]{2,0,1:T(8,128)(2,1)} %get-tuple-element.137, bf16[4,512,2,128]{3,1,2,0:T(8,128)(2,1)} %get-tuple-element.136, s32[]{:T(128)} %get-tuple-element.124), kind=kOutput, calls=%fused_computation.93.clone.1 | convolution fusion | flops 545261568 | bytes 10752512 | tf_op jit(solution)/shard_map/while/body/eval_jaxpr/sub | solution.py:26
  304.9 4.9 fusion.89
  311.5 7.7 %fusion.88 = (f32[2,512]{1,0:T(2,128)S(1)}, f32[2,512,2048]{2,1,0:T(8,128)}) fusion(pred[512,2048]{1,0:T(8,128)(4,1)S(1)} %broadcast_compare_fusion.2, bf16[2048,2,128]{2,0,1:T(8,128)(2,1)} %get-tuple-element.137, bf16[4,512,2,128]{3,1,2,0:T(8,128)(2,1)} %get-tuple-element.136, s32[]{:T(128)} %get-tuple-element.124), kind=kOutput, calls=%fused_computation.93.clone.1 | convolution fusion | flops 545261568 | bytes 10752512 | tf_op jit(solution)/shard_map/while/body/eval_jaxpr/sub | solution.py:26
  319.1 4.9 fusion.89
  327.5 7.0 %all-to-all-start.1 = ((bf16[8,256,256]{2,1,0:T(8,128)(2,1)}), bf16[8,256,256]{2,1,0:T(8,128)(2,1)S(1)}, u32[]{:S(2)}, u32[]{:S(2)}) async-start(bf16[8,256,256]{2,1,0:T(8,128)(2,1)} %reshape_reshape.3), calls=%async_computation.1 | async-start | bytes 2097152 | tf_op jit(solution)/shard_map/all_to_all | solution.py:104
  337.6 12.1 %all-to-all-done.1 = bf16[8,256,256]{2,1,0:T(8,128)(2,1)S(1)} async-done(((bf16[8,256,256]{2,1,0:T(8,128)(2,1)}), bf16[8,256,256]{2,1,0:T(8,128)(2,1)S(1)}, u32[]{:S(2)}, u32[]{:S(2)}) %all-to-all-start.1) | async-done | bytes 1048608 | tf_op jit(solution)/shard_map/all_to_all | solution.py:104
  349.7 10.6 %convert_reduce_fusion = f32[256,3200]{1,0:T(8,128)} fusion(bf16[8,256,256]{2,1,0:T(8,128)(2,1)S(1)} %all-to-all-done.1, bf16[8,256,3200]{2,1,0:T(8,128)(2,1)} %bitcast.91), kind=kOutput, calls=%fused_computation.24 | convolution fusion | flops 3374284800 | bytes 17432576 | tf_op jit(solution)/shard_map/gtc,gcd->gtd/dot_general | solution.py:106
  360.2 5.3 reduce_sum.69
  381.1 8.0 %all-to-all-start.2 = ((bf16[64,16,800]{2,0,1:T(8,128)(2,1)}), bf16[64,16,800]{2,0,1:T(8,128)(2,1)S(1)}, u32[]{:S(2)}, u32[]{:S(2)}) async-start(bf16[64,16,800]{2,0,1:T(8,128)(2,1)} %copy.31), calls=%async_computation.2 | async-start | bytes 3670016 | tf_op jit(solution)/shard_map/all_to_all | solution.py:128
  391.9 20.2 %all-to-all-done.2 = bf16[64,16,800]{2,0,1:T(8,128)(2,1)S(1)} async-done(((bf16[64,16,800]{2,0,1:T(8,128)(2,1)}), bf16[64,16,800]{2,0,1:T(8,128)(2,1)S(1)}, u32[]{:S(2)}, u32[]{:S(2)}) %all-to-all-start.2) | async-done | bytes 1638432 | tf_op jit(solution)/shard_map/all_to_all | solution.py:128
  413.4 19.2 %add_convert_fusion = bf16[16,64,6144]{2,1,0:T(8,128)(2,1)} fusion(f32[16,64]{1,0:T(8,128)S(1)} %broadcast_multiply_fusion, bf16[800,6144]{1,0:T(8,128)(2,1)} %param.25, bf16[16,64,800]{2,0,1:T(8,128)(2,1)S(1)} %fusion.34), kind=kOutput, calls=%fused_computation.25 | convolution fusion | flops 10078912512 | bytes 24055808 | tf_op jit(solution)/shard_map/dot_general | solution.py:139
  432.7 95.0 %reduce-scatter.2.cloned.1.call-done = bf16[64,6144]{1,0:T(8,128)(2,1)} async-done(((bf16[1024,6144]{1,0:T(8,128)(2,1)}), bf16[64,6144]{1,0:T(8,128)(2,1)}) %reduce-scatter.2.cloned.1.call-update) | async-done | bytes 786448 | tf_op jit(solution)/shard_map/reduce_scatter | solution.py:145
  527.6 5.2 fusion.52
  (78 shorter events, 47.5 us)
Async XLA Ops:
  6.5 2.0 copy-start
  16.1 203.8 %all-to-all-start = ((bf16[8,256,3200]{2,1,0:T(8,128)(2,1)}), bf16[8,256,3200]{2,1,0:T(8,128)(2,1)}, u32[]{:S(2)}, u32[]{:S(2)}) async-start(bf16[8,256,3200]{2,1,0:T(8,128)(2,1)} %stack.11), calls=%async_computation | async-start | bytes 26214400 | tf_op jit(solution)/shard_map/all_to_all | solution.py:65
  22.8 326.9 %all-gather.3.cloned.1.call-start = ((), (), s32[]{:S(2)}) async-start(), calls=%async_computation.5 | async-start | bytes 14745600 | tf_op jit(solution)/shard_map/all_gather | solution.py:105
  23.5 7.5 %copy-start.8 = (s32[1,256]{1,0:T(1,128)S(1)}, s32[1,256]{1,0:T(1,128)}, u32[]{:S(2)}) copy-start(s32[1,256]{1,0:T(1,128)} %param.21) | copy-start | bytes 3076
  23.5 7.5 %copy-start.7 = (f32[2,256]{1,0:T(2,128)S(1)}, f32[2,256]{1,0:T(2,128)}, u32[]{:S(2)}) copy-start(f32[2,256]{1,0:T(2,128)} %param.18) | copy-start | bytes 6148
  235.0 3.3 copy-start.2
  327.5 22.1 %all-to-all-start.1 = ((bf16[8,256,256]{2,1,0:T(8,128)(2,1)}), bf16[8,256,256]{2,1,0:T(8,128)(2,1)S(1)}, u32[]{:S(2)}, u32[]{:S(2)}) async-start(bf16[8,256,256]{2,1,0:T(8,128)(2,1)} %reshape_reshape.3), calls=%async_computation.1 | async-start | bytes 2097152 | tf_op jit(solution)/shard_map/all_to_all | solution.py:104
  334.5 2.8 copy-start.3
  334.5 2.9 copy-start.4
  360.2 5.3 copy-start.1
  360.2 5.3 copy-start.6
  381.1 8.6 %copy-start.9 = (s32[1,256]{1,0:T(1,128)S(1)}, s32[1,256]{1,0:T(1,128)}, u32[]{:S(2)}) copy-start(s32[1,256]{1,0:T(1,128)} %param.22) | copy-start | bytes 3076
  381.1 9.6 %copy-start.10 = (s32[16]{0:T(128)S(1)}, s32[16]{0:T(128)}, u32[]{:S(2)}) copy-start(s32[16]{0:T(128)} %param.27) | copy-start | bytes 196
  381.1 31.0 %all-to-all-start.2 = ((bf16[64,16,800]{2,0,1:T(8,128)(2,1)}), bf16[64,16,800]{2,0,1:T(8,128)(2,1)S(1)}, u32[]{:S(2)}, u32[]{:S(2)}) async-start(bf16[64,16,800]{2,0,1:T(8,128)(2,1)} %copy.31), calls=%async_computation.2 | async-start | bytes 3670016 | tf_op jit(solution)/shard_map/all_to_all | solution.py:128
  389.1 138.6 %reduce-scatter.2.cloned.1.call-start = ((), (), s32[]{:S(2)}) async-start(), calls=%async_computation.4 | async-start | bytes 13369344 | tf_op jit(solution)/shard_map/reduce_scatter | solution.py:145
  432.6 95.0 %copy-start.5 = (f32[6144]{0:T(1024)S(1)}, f32[6144]{0:T(1024)}, u32[]{:S(2)}) copy-start(f32[6144]{0:T(1024)} %param.26) | copy-start | bytes 73732
Sparse Core Ops, SparseCore 0:
  25.3 141.7 all-gather.2
  432.8 94.8 reduce-scatter.1
